TPU v7x, 512 devices: a whole 4x4x16 slice. The times are simulated.
512 devices in a mesh: dp: 4 (over y), head: 2 (over core), tile: 64 (over z, x).
Axes of the slice: x: 4, y: 4, z: 16, core: 2. Of those that a mesh axis runs over, the one named last changes fastest.
Arguments:
- tiles_in: bfloat16 [4, 16384, 2560], P('dp', 'tile'), may hold values from -6 to 6
- key_weight: bfloat16 [2560, 1280], P('tile', 'head'), may hold values from -0.125 to 0.125
- value_weight: bfloat16 [2560, 1280], P('tile', 'head'), may hold values from -0.125 to 0.125
- queries: bfloat16 [512, 1280], P(None, 'head'), may hold values from -300 to 300
- out_grad: bfloat16 [4, 512, 1280], P('dp', None, 'head'), may hold values from -1536 to 1536
- valid_count: int32 [4], P('dp'), may hold values from 4096 to 16384, as said below
- tile_mask: int32 [4, 16384], P('dp', 'tile'), may hold values 0 or 1
Outputs:
- tile_grad: bfloat16 [4, 16384, 2560], P('dp', 'tile', 'head')
Inputs may be any that keep to these rules, and one draw needn't show every extreme that they name: Some slide has valid_count equal to 16384.
All inputs are finite; a program needn't handle non-finite values. No bound on the sum of `tile_mask` on one device may be relied on, other than what follows from the above.
Results may differ from a plain program's by a relative error of at most 0.022.
Values may be sent and summed in bfloat16 or wider, within the bound.
No kernel may reach another device: no remote copies, remote signals or barrier semaphores. Data moves between devices by JAX's collectives and lax.ppermute only.
A program may use at most 64 MiB of HBM per device.

v0:
```python
import jax
import jax.numpy as jnp
from jax import lax
from jax.sharding import PartitionSpec as P

HDIM = 80
NEG_LARGE = -1e30


def per_device(tiles_in, key_weight, value_weight, queries, out_grad, valid_count, tile_mask):
    inv_scale = HDIM ** (-0.5)
    tile_dev = tiles_in.shape[1]
    group_width = queries.shape[1]
    heads_here = group_width // HDIM
    latents = queries.shape[0]
    local_tiles = tiles_in[0]
    positions = lax.axis_index("tile") * tile_dev + jnp.arange(tile_dev, dtype=jnp.int32)
    kept = (tile_mask[0] == 1) | (positions == 0)
    valid = ((positions < valid_count[0]) & kept)[None, None, :]
    full_key, full_value = (
        lax.all_gather(key_weight, "tile", axis=0, tiled=True),
        lax.all_gather(value_weight, "tile", axis=0, tiled=True),
    )
    keys = jnp.dot(local_tiles, full_key, preferred_element_type=jnp.float32)
    values = jnp.dot(local_tiles, full_value, preferred_element_type=jnp.float32).astype(
        jnp.bfloat16
    )
    query_heads = queries.reshape(latents, heads_here, HDIM)
    query_wide = queries.astype(jnp.float32).reshape(latents, heads_here, HDIM)
    key_heads = keys.reshape(tile_dev, heads_here, HDIM)
    value_heads = values.reshape(tile_dev, heads_here, HDIM)
    grad_heads = out_grad[0].reshape(latents, heads_here, HDIM)
    scores = (
        jnp.einsum(
            "lhd,thd->hlt",
            query_wide,
            key_heads,
            precision=lax.Precision.HIGHEST,
            preferred_element_type=jnp.float32,
        )
        * inv_scale
    )
    prob_grad = jnp.einsum(
        "lhd,thd->hlt", grad_heads, value_heads, preferred_element_type=jnp.float32
    )
    local_max = jnp.max(jnp.where(valid, scores, NEG_LARGE), axis=2)
    row_max = lax.pmax(local_max, "tile")
    expd = jnp.where(valid, jnp.exp(scores - row_max[:, :, None]), 0.0)
    total, weighted = lax.psum((jnp.sum(expd, axis=2), jnp.sum(expd * prob_grad, axis=2)), "tile")
    delta = weighted / total
    probs = expd / total[:, :, None]
    dscore = (inv_scale * probs * (prob_grad - delta[:, :, None])).astype(jnp.bfloat16)
    value_grad = (
        jnp.einsum(
            "hlt,lhd->thd",
            probs.astype(jnp.bfloat16),
            grad_heads,
            preferred_element_type=jnp.float32,
        )
        .astype(jnp.bfloat16)
        .reshape(tile_dev, group_width)
    )
    key_grad = (
        jnp.einsum("hlt,lhd->thd", dscore, query_heads, preferred_element_type=jnp.float32)
        .astype(jnp.bfloat16)
        .reshape(tile_dev, group_width)
    )
    partial_sum = jnp.einsum("tc,rc->tr", key_grad, full_key, preferred_element_type=jnp.float32)
    partial_sum = partial_sum + jnp.einsum(
        "tc,rc->tr", value_grad, full_value, preferred_element_type=jnp.float32
    )
    rounded = partial_sum.astype(jnp.bfloat16)
    summed = lax.psum_scatter(rounded[None], "head", scatter_dimension=2, tiled=True).astype(
        jnp.float32
    )
    return summed.astype(jnp.bfloat16)


def solution(mesh):
    return jax.shard_map(
        per_device,
        mesh=mesh,
        in_specs=(
            P("dp", "tile", None),
            P("tile", "head"),
            P("tile", "head"),
            P(None, "head"),
            P("dp", None, "head"),
            P("dp"),
            P("dp", "tile"),
        ),
        out_specs=P("dp", "tile", "head"),
        check_vma=False,
    )
```

profile of v0, /device:TPU:1, one launch (start us, length us, event | category | flops | bytes accessed | tf_op | source)
XLA Modules:
  0.0 901.9 jit_solution(17040804668018746320)
XLA Ops:
  6.5 0.0 copy-start
  6.5 0.0 all-gather.5.cloned.1.call-start
  6.5 0.7 all-gather.5.cloned.1.call-update
  7.3 0.0 all-gather.3.cloned.1.call-start
  7.3 0.7 all-gather.3.cloned.1.call-update
  8.0 0.0 reduce-scatter.2.cloned.1.call-start
  8.7 1.3 copy.22
  10.0 1.3 copy.24
  11.4 0.7 compare_reduce_fusion
  12.1 139.2 %all-gather.5.cloned.1.call-done = bf16[2560,640]{1,0:T(8,128)(2,1)} async-done(((bf16[40,640]{1,0:T(8,128)(2,1)}), bf16[2560,640]{1,0:T(8,128)(2,1)}) %all-gather.5.cloned.1.call-update) | async-done | bytes 3276816 | tf_op jit(solution)/shard_map/all_gather | solution.py:22
  151.3 0.0 copy-done
  151.3 3.1 fusion.15
  154.4 0.2 copy.23
  154.6 138.5 %all-gather.3.cloned.1.call-done = bf16[2560,640]{1,0:T(8,128)(2,1)} async-done(((bf16[40,640]{1,0:T(8,128)(2,1)}), bf16[2560,640]{1,0:T(8,128)(2,1)}) %all-gather.3.cloned.1.call-update) | async-done | bytes 3276816 | tf_op jit(solution)/shard_map/all_gather | solution.py:21
  293.1 5.7 copy.21
  298.8 3.0 fusion.11
  301.8 4.2 select_reduce_fusion
  305.9 221.1 %pmax.7 = f32[8,512]{1,0:T(8,128)S(1)} all-reduce(f32[8,512]{1,0:T(8,128)S(1)} %get-tuple-element.9), channel_id=1, replica_groups=mesh['dp'=4,'head'=2,'tile'=64] {'tile'}, use_global_device_ids=true, to_apply=%region_1.2 | all-reduce | flops 4096 | bytes 32768 | tf_op jit(solution)/shard_map/pmax | solution.py:47
  527.0 5.7 bitcast_reduce_fusion
  532.7 219.7 %all-reduce = (f32[8,512]{1,0:T(8,128)S(1)}, f32[8,512]{1,0:T(8,128)S(1)}) all-reduce(f32[8,512]{1,0:T(8,128)S(1)} %get-tuple-element.6, f32[8,512]{1,0:T(8,128)S(1)} %get-tuple-element.5), channel_id=1, replica_groups=mesh['dp'=4,'head'=2,'tile'=64] {'tile'}, use_global_device_ids=true, to_apply=%region_5.6 | all-reduce | flops 8192 | bytes 65536 | tf_op jit(solution)/shard_map/psum | solution.py:49
  752.4 0.0 copy-start.1
  752.4 0.0 copy-start.3
  752.4 3.5 fusion.18
  755.8 0.0 copy-done.1
  755.9 1.2 copy-done.3
  757.1 0.0 copy-start.2
  757.1 1.6 fusion.21
  758.7 0.0 copy-start.4
  758.7 0.4 copy-done.2
  759.0 1.2 fusion.25
  760.3 0.4 copy-done.4
  760.7 2.4 fusion.4
  763.0 0.0 reduce-scatter.2.cloned.1.call-update
  763.1 132.3 %reduce-scatter.2.cloned.1.call-done = bf16[1,256,1280]{2,1,0:T(8,128)(2,1)} async-done(((bf16[1,256,2560]{2,1,0:T(8,128)(2,1)}), bf16[1,256,1280]{2,1,0:T(8,128)(2,1)}) %reduce-scatter.2.cloned.1.call-update) | async-done | bytes 655376 | tf_op jit(solution)/shard_map/reduce_scatter | solution.py:73
  (2 shorter events, 0.0 us)
Async XLA Ops:
  6.5 144.7 %copy-start = (bf16[1,256,2560]{2,1,0:T(8,128)(2,1)S(1)}, bf16[1,256,2560]{2,1,0:T(8,128)(2,1)}, u32[]{:S(2)}) copy-start(bf16[1,256,2560]{2,1,0:T(8,128)(2,1)} %param.7) | copy-start | bytes 3932164
  6.5 144.7 %all-gather.5.cloned.1.call-start = ((), (), s32[]{:S(2)}) async-start(), calls=%async_computation.2 | async-start | bytes 3328000 | tf_op jit(solution)/shard_map/all_gather | solution.py:22
  7.3 285.8 %all-gather.3.cloned.1.call-start = ((), (), s32[]{:S(2)}) async-start(), calls=%async_computation.1 | async-start | bytes 3328000 | tf_op jit(solution)/shard_map/all_gather | solution.py:21
  8.0 887.3 %reduce-scatter.2.cloned.1.call-start = ((), (), s32[]{:S(2)}) async-start(), calls=%async_computation.3 | async-start | bytes 1966080 | tf_op jit(solution)/shard_map/reduce_scatter | solution.py:73
  752.4 3.5 copy-start.1
  752.4 4.7 copy-start.3
  757.1 1.9 copy-start.2
  758.7 2.0 copy-start.4
Sparse Core Ops, SparseCore 0:
  10.3 140.9 all-gather.4
  154.2 138.8 all-gather.2
  763.2 132.0 reduce-scatter.1
where the time goes:
time: 902 us
  blocking collectives  441 us (49%)
  waiting for transfers between devices  411 us (46%)
  matrix products  24.5 us (3%)
  between operations  13.8 us (2%)
  local copies, waits for them, and re-layouts  10.5 us (1%)
    pmax x1, blocking collectives, per_device(): row_max = lax.pmax(local_max, 'tile')  221 us
    psum x1, blocking collectives, per_device(): lax.psum((jnp.sum(expd, axis=2), jnp.sum(expd * prob_grad, axis=2)), 'tile')  220 us
    all_gather x1, waiting for transfers between devices, per_device(): lax.all_gather(value_weight, 'tile', axis=0, tiled=True)  139 us
    all_gather x1, waiting for transfers between devices, per_device(): lax.all_gather(key_weight, 'tile', axis=0, tiled=True)  139 us
    reduce_scatter x1, waiting for transfers between devices, per_device(): lax.psum_scatter(rounded[None], 'head', scatter_dimension=2, tiled=True)  132 us
  transfers between devices with their start and end apart: 3, of which 3 were waited for; matrix products, arithmetic and copies ran while one was open for 1% of the time, Pallas kernels for 0%

commit v1 on v0

--- a/solution.py
+++ b/solution.py
@@ -19,7 +19,9 @@
     valid = ((positions < valid_count[0]) & kept)[None, None, :]
     full_key, full_value = (
         lax.all_gather(key_weight, "tile", axis=0, tiled=True),
-        lax.all_gather(value_weight, "tile", axis=0, tiled=True),
+        jnp.concatenate(
+            lax.all_to_all(jnp.stack([value_weight] * lax.axis_size("tile")), "tile", 0, 0), axis=0
+        ),
     )
     keys = jnp.dot(local_tiles, full_key, preferred_element_type=jnp.float32)
     values = jnp.dot(local_tiles, full_value, preferred_element_type=jnp.float32).astype(

time: 902 us -> 825 us (0.915)
  waiting for transfers between devices: 411 us -> 311 us
  starting transfers between devices: 0.08 us -> 19.6 us
    all_gather x1 -> x0, waiting for transfers between devices: 139 us -> none  [per_device(): lax.all_gather(value_weight, 'tile', axis=0, tiled=True)]
    all_gather x1, waiting for transfers between devices: 139 us -> 180 us  [per_device(): lax.all_gather(key_weight, 'tile', axis=0, tiled=True)]
    all_to_all x0 -> x1, starting transfers between devices: none -> 19.5 us  [per_device(): lax.all_to_all(jnp.stack([value_weight] * lax.axis_size('tile')), 'tile',...]
  transfers between devices with their start and end apart: 3 -> 3, of which waited for: 3 -> 2; matrix products, arithmetic and copies ran while one was open for 1% -> 2% of each run, Pallas kernels for 0% -> 0%
where the time goes in v1:
time: 825 us
  blocking collectives  442 us (54%)
  waiting for transfers between devices  311 us (38%)
  matrix products  26.5 us (3%)
  starting transfers between devices  19.6 us (2%)
  between operations  14.2 us (2%)
  local copies, waits for them, and re-layouts  10.9 us (1%)
    pmax x1, blocking collectives, per_device(): row_max = lax.pmax(local_max, 'tile')  223 us
    psum x1, blocking collectives, per_device(): lax.psum((jnp.sum(expd, axis=2), jnp.sum(expd * prob_grad, axis=2)), 'tile')  220 us
    all_gather x1, waiting for transfers between devices, per_device(): lax.all_gather(key_weight, 'tile', axis=0, tiled=True)  180 us
    reduce_scatter x1, waiting for transfers between devices, per_device(): lax.psum_scatter(rounded[None], 'head', scatter_dimension=2, tiled=True)  130 us
    all_to_all x1, starting transfers between devices, per_device(): lax.all_to_all(jnp.stack([value_weight] * lax.axis_size('tile')), 'tile',...  19.5 us
  transfers between devices with their start and end apart: 3, of which 2 were waited for; matrix products, arithmetic and copies ran while one was open for 2% of the time, Pallas kernels for 0%

profile of v1, /device:TPU:1, one launch (start us, length us, event | category | flops | bytes accessed | tf_op | source)
XLA Modules:
  0.0 824.7 jit_solution(8546799551818420046)
XLA Ops:
  6.5 0.0 copy-start
  6.5 0.0 copy-start.4
  6.5 2.9 stack.2
  9.4 0.0 copy-start.5
  9.5 0.0 copy-start.6
  9.5 19.5 %all-to-all-start = ((bf16[64,40,640]{2,1,0:T(8,128)(2,1)}), bf16[64,40,640]{2,1,0:T(8,128)(2,1)}, u32[]{:S(2)}, u32[]{:S(2)}) async-start(bf16[64,40,640]{2,1,0:T(8,128)(2,1)} %stack.2), calls=%async_computation | async-start | bytes 6553600 | tf_op jit(solution)/shard_map/all_to_all | solution.py:23
  28.9 0.0 all-gather.2.cloned.1.call-start
  29.0 0.7 all-gather.2.cloned.1.call-update
  29.7 0.0 reduce-scatter.2.cloned.1.call-start
  30.4 0.0 copy-done.4
  30.4 0.3 copy.22
  30.6 0.0 copy-done.5
  30.6 0.3 copy.24
  30.9 0.0 copy-done.6
  31.0 180.3 %all-gather.2.cloned.1.call-done = bf16[2560,640]{1,0:T(8,128)(2,1)} async-done(((bf16[40,640]{1,0:T(8,128)(2,1)}), bf16[2560,640]{1,0:T(8,128)(2,1)}) %all-gather.2.cloned.1.call-update) | async-done | bytes 3276816 | tf_op jit(solution)/shard_map/all_gather | solution.py:21
  211.3 5.7 copy.21
  217.0 0.0 copy-done
  217.0 3.0 fusion.11
  219.9 4.2 select_reduce_fusion
  224.1 222.8 %pmax.7 = f32[8,512]{1,0:T(8,128)S(1)} all-reduce(f32[8,512]{1,0:T(8,128)S(1)} %get-tuple-element.9), channel_id=1, replica_groups=mesh['dp'=4,'head'=2,'tile'=64] {'tile'}, use_global_device_ids=true, to_apply=%region_1.2 | all-reduce | flops 4096 | bytes 32768 | tf_op jit(solution)/shard_map/pmax | solution.py:49
  446.9 0.0 all-to-all-done
  446.9 3.1 fusion.15
  450.0 0.2 copy.23
  450.2 5.7 bitcast_reduce_fusion
  455.9 219.6 %all-reduce = (f32[8,512]{1,0:T(8,128)S(1)}, f32[8,512]{1,0:T(8,128)S(1)}) all-reduce(f32[8,512]{1,0:T(8,128)S(1)} %get-tuple-element.6, f32[8,512]{1,0:T(8,128)S(1)} %get-tuple-element.5), channel_id=1, replica_groups=mesh['dp'=4,'head'=2,'tile'=64] {'tile'}, use_global_device_ids=true, to_apply=%region_5.6 | all-reduce | flops 8192 | bytes 65536 | tf_op jit(solution)/shard_map/psum | solution.py:51
  675.5 0.0 copy-start.1
  675.5 0.0 copy-start.3
  675.5 3.5 fusion.18
  679.0 0.0 copy-done.1
  679.0 1.2 copy-done.3
  680.2 0.0 copy-start.2
  680.2 1.6 fusion.21
  681.8 0.4 copy-done.2
  682.1 1.2 fusion.25
  683.4 4.3 fusion.4
  687.7 0.0 reduce-scatter.2.cloned.1.call-update
  687.7 130.2 %reduce-scatter.2.cloned.1.call-done = bf16[1,256,1280]{2,1,0:T(8,128)(2,1)} async-done(((bf16[1,256,2560]{2,1,0:T(8,128)(2,1)}), bf16[1,256,1280]{2,1,0:T(8,128)(2,1)}) %reduce-scatter.2.cloned.1.call-update) | async-done | bytes 655376 | tf_op jit(solution)/shard_map/reduce_scatter | solution.py:75
  (3 shorter events, 0.0 us)
Async XLA Ops:
  6.5 210.4 %copy-start = (bf16[1,256,2560]{2,1,0:T(8,128)(2,1)S(1)}, bf16[1,256,2560]{2,1,0:T(8,128)(2,1)}, u32[]{:S(2)}) copy-start(bf16[1,256,2560]{2,1,0:T(8,128)(2,1)} %param.7) | copy-start | bytes 3932164
  6.5 23.8 %copy-start.4 = (bf16[512,640]{1,0:T(8,128)(2,1)S(1)}, bf16[512,640]{1,0:T(8,128)(2,1)}, u32[]{:S(2)}) copy-start(bf16[512,640]{1,0:T(8,128)(2,1)} %param.10) | copy-start | bytes 1966084
  9.4 21.2 %copy-start.5 = (bf16[1,512,640]{2,1,0:T(8,128)(2,1)S(1)}, bf16[1,512,640]{2,1,0:T(8,128)(2,1)}, u32[]{:S(2)}) copy-start(bf16[1,512,640]{2,1,0:T(8,128)(2,1)} %param.11) | copy-start | bytes 1966084
  9.5 21.5 %copy-start.6 = (s32[1,256]{1,0:T(1,128)S(1)}, s32[1,256]{1,0:T(1,128)}, u32[]{:S(2)}) copy-start(s32[1,256]{1,0:T(1,128)} %param.13) | copy-start | bytes 3076
  9.5 437.5 %all-to-all-start = ((bf16[64,40,640]{2,1,0:T(8,128)(2,1)}), bf16[64,40,640]{2,1,0:T(8,128)(2,1)}, u32[]{:S(2)}, u32[]{:S(2)}) async-start(bf16[64,40,640]{2,1,0:T(8,128)(2,1)} %stack.2), calls=%async_computation | async-start | bytes 6553600 | tf_op jit(solution)/shard_map/all_to_all | solution.py:23
  28.9 182.3 %all-gather.2.cloned.1.call-start = ((), (), s32[]{:S(2)}) async-start(), calls=%async_computation.2 | async-start | bytes 3328000 | tf_op jit(solution)/shard_map/all_gather | solution.py:21
  29.7 788.2 %reduce-scatter.2.cloned.1.call-start = ((), (), s32[]{:S(2)}) async-start(), calls=%async_computation.3 | async-start | bytes 1966080 | tf_op jit(solution)/shard_map/reduce_scatter | solution.py:75
  675.5 3.5 copy-start.1
  675.5 4.7 copy-start.3
  680.2 1.9 copy-start.2
Sparse Core Ops, SparseCore 0:
  32.7 178.5 all-gather.1
  687.8 130.0 reduce-scatter.1

commit v2 on v0

--- a/solution.py
+++ b/solution.py
@@ -5,6 +5,12 @@
 
 HDIM = 80
 NEG_LARGE = -1e30
+
+
+def tiled_gather(x, axis, dim):
+    size = lax.axis_size(axis)
+    repeats = [size if d == dim else 1 for d in range(x.ndim)]
+    return lax.all_to_all(jnp.tile(x, repeats), axis, split_axis=dim, concat_axis=dim, tiled=True)
 
 
 def per_device(tiles_in, key_weight, value_weight, queries, out_grad, valid_count, tile_mask):
@@ -18,7 +24,7 @@
     kept = (tile_mask[0] == 1) | (positions == 0)
     valid = ((positions < valid_count[0]) & kept)[None, None, :]
     full_key, full_value = (
-        lax.all_gather(key_weight, "tile", axis=0, tiled=True),
+        tiled_gather(key_weight, "tile", 0),
         lax.all_gather(value_weight, "tile", axis=0, tiled=True),
     )
     keys = jnp.dot(local_tiles, full_key, preferred_element_type=jnp.float32)

time: 902 us -> 825 us (0.915)
  waiting for transfers between devices: 411 us -> 311 us
  starting transfers between devices: 0.08 us -> 19.6 us
    all_gather x1 -> x0, waiting for transfers between devices: 139 us -> none  [per_device(): lax.all_gather(key_weight, 'tile', axis=0, tiled=True)]
    all_gather x1, waiting for transfers between devices: 139 us -> 180 us  [per_device(): lax.all_gather(value_weight, 'tile', axis=0, tiled=True)]
    all_to_all x0 -> x1, starting transfers between devices: none -> 19.5 us  [tiled_gather(): lax.all_to_all(jnp.tile(x, repeats), axis, split_axis=dim, concat_axis=di...]
  transfers between devices with their start and end apart: 3 -> 3, of which waited for: 3 -> 2; matrix products, arithmetic and copies ran while one was open for 1% -> 0% of each run, Pallas kernels for 0% -> 0%
where the time goes in v2:
time: 825 us
  blocking collectives  442 us (54%)
  waiting for transfers between devices  311 us (38%)
  matrix products  26.7 us (3%)
  starting transfers between devices  19.6 us (2%)
  between operations  14.2 us (2%)
  local copies, waits for them, and re-layouts  10.5 us (1%)
    pmax x1, blocking collectives, per_device(): row_max = lax.pmax(local_max, 'tile')  223 us
    psum x1, blocking collectives, per_device(): lax.psum((jnp.sum(expd, axis=2), jnp.sum(expd * prob_grad, axis=2)), 'tile')  220 us
    all_gather x1, waiting for transfers between devices, per_device(): lax.all_gather(value_weight, 'tile', axis=0, tiled=True)  180 us
    reduce_scatter x1, waiting for transfers between devices, per_device(): lax.psum_scatter(rounded[None], 'head', scatter_dimension=2, tiled=True)  130 us
    all_to_all x1, starting transfers between devices, tiled_gather(): lax.all_to_all(jnp.tile(x, repeats), axis, split_axis=dim, concat_axis=di...  19.5 us
  transfers between devices with their start and end apart: 3, of which 2 were waited for; matrix products, arithmetic and copies ran while one was open for 0% of the time, Pallas kernels for 0%

profile of v2, /device:TPU:1, one launch (start us, length us, event | category | flops | bytes accessed | tf_op | source)
XLA Modules:
  0.0 824.6 jit_solution(3423262271884742137)
XLA Ops:
  6.5 0.0 copy-start
  6.5 0.0 copy-start.4
  6.5 2.9 tile.2
  9.4 0.0 copy-start.5
  9.4 0.0 copy-start.6
  9.4 19.5 %all-to-all-start = ((bf16[64,40,640]{2,1,0:T(8,128)(2,1)}), bf16[64,40,640]{2,1,0:T(8,128)(2,1)}, u32[]{:S(2)}, u32[]{:S(2)}) async-start(bf16[64,40,640]{2,1,0:T(8,128)(2,1)} %tile.2), calls=%async_computation | async-start | bytes 6553600 | tf_op jit(solution)/shard_map/all_to_all | solution.py:13
  28.9 0.0 all-gather.2.cloned.1.call-start
  29.0 0.7 all-gather.2.cloned.1.call-update
  29.6 0.0 reduce-scatter.2.cloned.1.call-start
  30.3 0.0 copy-done.4
  30.4 0.3 copy.22
  30.6 0.0 copy-done.5
  30.6 0.3 copy.24
  30.9 0.0 copy-done.6
  30.9 180.3 %all-gather.2.cloned.1.call-done = bf16[2560,640]{1,0:T(8,128)(2,1)} async-done(((bf16[40,640]{1,0:T(8,128)(2,1)}), bf16[2560,640]{1,0:T(8,128)(2,1)}) %all-gather.2.cloned.1.call-update) | async-done | bytes 3276816 | tf_op jit(solution)/shard_map/all_gather | solution.py:28
  211.3 0.0 copy-done
  211.3 3.1 fusion.15
  214.4 0.2 copy.23
  214.5 0.0 all-to-all-done
  214.6 5.7 copy.21
  220.2 3.0 fusion.11
  223.2 4.2 select_reduce_fusion
  227.4 222.8 %pmax.7 = f32[8,512]{1,0:T(8,128)S(1)} all-reduce(f32[8,512]{1,0:T(8,128)S(1)} %get-tuple-element.9), channel_id=1, replica_groups=mesh['dp'=4,'head'=2,'tile'=64] {'tile'}, use_global_device_ids=true, to_apply=%region_1.2 | all-reduce | flops 4096 | bytes 32768 | tf_op jit(solution)/shard_map/pmax | solution.py:53
  450.2 5.7 bitcast_reduce_fusion
  455.9 219.6 %all-reduce = (f32[8,512]{1,0:T(8,128)S(1)}, f32[8,512]{1,0:T(8,128)S(1)}) all-reduce(f32[8,512]{1,0:T(8,128)S(1)} %get-tuple-element.6, f32[8,512]{1,0:T(8,128)S(1)} %get-tuple-element.5), channel_id=1, replica_groups=mesh['dp'=4,'head'=2,'tile'=64] {'tile'}, use_global_device_ids=true, to_apply=%region_5.6 | all-reduce | flops 8192 | bytes 65536 | tf_op jit(solution)/shard_map/psum | solution.py:55
  675.5 0.0 copy-start.1
  675.5 0.0 copy-start.2
  675.5 3.5 fusion.18
  678.9 0.0 copy-done.1
  679.0 1.2 copy-done.2
  680.2 1.6 fusion.21
  681.8 0.0 copy-start.3
  681.8 3.3 fusion.25
  685.1 0.0 copy-done.3
  685.1 2.4 fusion.4
  687.5 0.0 reduce-scatter.2.cloned.1.call-update
  687.5 130.2 %reduce-scatter.2.cloned.1.call-done = bf16[1,256,1280]{2,1,0:T(8,128)(2,1)} async-done(((bf16[1,256,2560]{2,1,0:T(8,128)(2,1)}), bf16[1,256,1280]{2,1,0:T(8,128)(2,1)}) %reduce-scatter.2.cloned.1.call-update) | async-done | bytes 655376 | tf_op jit(solution)/shard_map/reduce_scatter | solution.py:79
  (3 shorter events, 0.0 us)
Async XLA Ops:
  6.5 204.7 %copy-start = (bf16[1,256,2560]{2,1,0:T(8,128)(2,1)S(1)}, bf16[1,256,2560]{2,1,0:T(8,128)(2,1)}, u32[]{:S(2)}) copy-start(bf16[1,256,2560]{2,1,0:T(8,128)(2,1)} %param.7) | copy-start | bytes 3932164
  6.5 23.8 %copy-start.4 = (bf16[512,640]{1,0:T(8,128)(2,1)S(1)}, bf16[512,640]{1,0:T(8,128)(2,1)}, u32[]{:S(2)}) copy-start(bf16[512,640]{1,0:T(8,128)(2,1)} %param.10) | copy-start | bytes 1966084
  9.4 21.2 %copy-start.5 = (bf16[1,512,640]{2,1,0:T(8,128)(2,1)S(1)}, bf16[1,512,640]{2,1,0:T(8,128)(2,1)}, u32[]{:S(2)}) copy-start(bf16[1,512,640]{2,1,0:T(8,128)(2,1)} %param.11) | copy-start | bytes 1966084
  9.4 21.5 %copy-start.6 = (s32[1,256]{1,0:T(1,128)S(1)}, s32[1,256]{1,0:T(1,128)}, u32[]{:S(2)}) copy-start(s32[1,256]{1,0:T(1,128)} %param.13) | copy-start | bytes 3076
  9.4 205.1 %all-to-all-start = ((bf16[64,40,640]{2,1,0:T(8,128)(2,1)}), bf16[64,40,640]{2,1,0:T(8,128)(2,1)}, u32[]{:S(2)}, u32[]{:S(2)}) async-start(bf16[64,40,640]{2,1,0:T(8,128)(2,1)} %tile.2), calls=%async_computation | async-start | bytes 6553600 | tf_op jit(solution)/shard_map/all_to_all | solution.py:13
  28.9 182.3 %all-gather.2.cloned.1.call-start = ((), (), s32[]{:S(2)}) async-start(), calls=%async_computation.2 | async-start | bytes 3328000 | tf_op jit(solution)/shard_map/all_gather | solution.py:28
  29.6 788.1 %reduce-scatter.2.cloned.1.call-start = ((), (), s32[]{:S(2)}) async-start(), calls=%async_computation.3 | async-start | bytes 1966080 | tf_op jit(solution)/shard_map/reduce_scatter | solution.py:79
  675.5 3.5 copy-start.1
  675.5 4.7 copy-start.2
  681.8 3.4 copy-start.3
Sparse Core Ops, SparseCore 0:
  32.7 178.5 all-gather.1
  687.6 130.0 reduce-scatter.1
